TPU v7x, 32 devices: a whole 2x2x4 slice. The times are simulated.
32 devices in a mesh: region: 32 (over z, y, x, core).
Axes of the slice: x: 2, y: 2, z: 4, core: 2. Of those that a mesh axis runs over, the one named last changes fastest.
Arguments:
- gaussians: float32 [32, 9, 4096], P('region')
- depth: int32 [32, 512, 8], P('region'), may hold values from 0 to 7, each once within a row
- coverage: int32 [32, 512], P('region'), may hold values 0 or 1
- flips: int32 [512, 31], replicated, may hold values 0 or 1
- features: bfloat16 [131072, 384], P('region'), may hold values from -6 to 6
- w_first: bfloat16 [384, 384], replicated, may hold values from -0.3125 to 0.3125
- b_first: float32 [384], replicated, may hold values from -3 to 3
- w_second: bfloat16 [384], replicated, may hold values from -0.3125 to 0.3125
- target: float32 [3, 131072], P(None, 'region'), may hold values from 0 to 1
Outputs:
- pixel_loss: float32 [131072], P('region')
- splat_grads: float32 [32, 9, 4096], P('region')
Inputs may be any that keep to these rules, and one draw needn't show every extreme that they name: Each tile's 8 depth ranks of one region are a permutation of 0 to 7.
All inputs are finite; a program needn't handle non-finite values. No bound on the sum of `coverage` on one device may be relied on, other than what follows from the above.
Results may differ from a plain program's by a relative error of at most 0.0022.
Values sent between devices are 32-bit elements; how exact they have to be, the bound alone decides.
A program may use at most 64 MiB of HBM per device.

v0:
```python
import functools

import jax
import jax.numpy as jnp
from jax import lax
from jax.experimental import pallas as pl
from jax.experimental.pallas import tpu as pltpu
from jax.sharding import PartitionSpec as P

TSIDE = 16
LANES = 128
NPAR = 10
LOG2E = 1.4426950408889634
HI = lax.Precision.HIGHEST


def render_kernel(
    x_ref, flip_ref, wanted_ref, spread_ref, loss_ref, grad_ref,
    d_ref, ex_ref, a_ref, t_ref, tree_ref, gtree_ref, mbuf, red_ref,
):
    regions, group = x_ref.shape[1:]
    splats = 8
    rows = wanted_ref.shape[1]
    nv = rows // 8
    stripe_tiles = group // splats
    span = LANES // stripe_tiles
    inner = regions - 1

    sub = lax.broadcasted_iota(jnp.int32, (8, LANES), 0)
    lane = lax.broadcasted_iota(jnp.int32, (8, LANES), 1)
    pix = sub * span + (lane & (span - 1))
    xpos = (pix & (TSIDE - 1)).astype(jnp.float32) + 0.5
    ypos = [((pix + 8 * v * span) // TSIDE).astype(jnp.float32) + 0.5 for v in range(nv)]
    vs = [slice(8 * v, 8 * v + 8) for v in range(nv)]

    spread_in = (
        lax.broadcasted_iota(jnp.int32, (group, LANES), 0) // splats
        == lax.broadcasted_iota(jnp.int32, (group, LANES), 1) // span
    ).astype(jnp.float32)
    gather_out = (
        lax.broadcasted_iota(jnp.int32, (LANES, group), 0) // span
        == lax.broadcasted_iota(jnp.int32, (LANES, group), 1) // splats
    ).astype(jnp.float32)
    rank_row = lax.broadcasted_iota(jnp.int32, (splats, group), 0).astype(jnp.float32)

    rho = 0.9 * jnp.tanh(x_ref[4])
    norm = lax.rsqrt(1.0 - rho * rho)
    d_ref[0] = x_ref[0]
    d_ref[1] = x_ref[1]
    d_ref[2] = jnp.exp(-x_ref[2])
    d_ref[3] = jnp.exp(-x_ref[3])
    d_ref[4] = norm
    d_ref[5] = rho * norm
    d_ref[6] = 0.99 * jax.nn.sigmoid(x_ref[5]) * x_ref[10]
    for k in range(3):
        d_ref[7 + k] = jax.nn.sigmoid(x_ref[6 + k])

    def expand(r, carry):
        mask = x_ref[9, pl.ds(r, 1), :] == rank_row
        picked = [
            jnp.where(mask, jnp.broadcast_to(d_ref[p, pl.ds(r, 1), :], (splats, group)), 0.0)
            for p in range(NPAR)
        ]
        ex_ref[r] = jnp.dot(
            jnp.concatenate(picked, 0), spread_in, precision=HI, preferred_element_type=jnp.float32
        )
        return carry

    lax.fori_loop(0, regions, expand, 0, unroll=2)

    def row(r, p, s):
        return ex_ref[r, pl.ds(p * splats + s, 1), :]

    def forward(r, carry):
        trans = [jnp.ones((8, LANES), jnp.float32)] * nv
        color = [[jnp.zeros((8, LANES), jnp.float32)] * nv for _ in range(3)]
        for s in range(splats):
            u = (xpos - row(r, 0, s)) * row(r, 2, s)
            us = u * row(r, 4, s)
            m_y, inv_y, skew, op = row(r, 1, s), row(r, 3, s), row(r, 5, s), row(r, 6, s)
            ks = [row(r, 7 + k, s) for k in range(3)]
            for v in range(nv):
                w = (ypos[v] - m_y) * inv_y
                p = us - skew * w
                alpha = op * jnp.exp2((p * p + w * w) * (-0.5 * LOG2E))
                a_ref[r * splats + s, vs[v]] = alpha
                t_ref[r * splats + s, vs[v]] = trans[v]
                weight = trans[v] * alpha
                for k in range(3):
                    color[k][v] = color[k][v] + weight * ks[k]
                trans[v] = trans[v] * (1.0 - alpha)
        for v in range(nv):
            for k in range(3):
                tree_ref[inner + r, k, vs[v]] = color[k][v]
            tree_ref[inner + r, 3, vs[v]] = trans[v]
        return carry

    lax.fori_loop(0, regions, forward, 0)

    def merge(i, carry):
        n = inner - 1 - i
        flip = jnp.broadcast_to(flip_ref[n], (8, LANES)) > 0.0
        for v in range(nv):
            low = [tree_ref[2 * n + 1, k, vs[v]] for k in range(4)]
            high = [tree_ref[2 * n + 2, k, vs[v]] for k in range(4)]
            front = [jnp.where(flip, h, l) for l, h in zip(low, high)]
            back = [jnp.where(flip, l, h) for l, h in zip(low, high)]
            for k in range(3):
                tree_ref[n, k, vs[v]] = front[k] + front[3] * back[k]
            tree_ref[n, 3, vs[v]] = front[3] * back[3]
        return carry

    lax.fori_loop(0, inner, merge, 0)

    for v in range(nv):
        spread = spread_ref[vs[v]]
        inv_square = 1.0 / (spread * spread)
        clear = tree_ref[0, 3, vs[v]]
        residual = [tree_ref[0, k, vs[v]] + clear - wanted_ref[k, vs[v]] for k in range(3)]
        total = residual[0] * residual[0] + residual[1] * residual[1] + residual[2] * residual[2]
        loss_ref[vs[v]] = 0.5 * total * inv_square + jnp.log(spread)
        gs = [res * inv_square for res in residual]
        for k in range(3):
            gtree_ref[0, k, vs[v]] = gs[k]
        gtree_ref[0, 3, vs[v]] = gs[0] + gs[1] + gs[2]

    def split(n, carry):
        flip = jnp.broadcast_to(flip_ref[n], (8, LANES)) > 0.0
        for v in range(nv):
            low = [tree_ref[2 * n + 1, k, vs[v]] for k in range(4)]
            high = [tree_ref[2 * n + 2, k, vs[v]] for k in range(4)]
            g = [gtree_ref[n, k, vs[v]] for k in range(4)]
            front_t = jnp.where(flip, high[3], low[3])
            back = [jnp.where(flip, l, h) for l, h in zip(low, high)]
            g_front_t = g[0] * back[0] + g[1] * back[1] + g[2] * back[2] + g[3] * back[3]
            for k in range(4):
                g_front = g[k] if k < 3 else g_front_t
                g_back = front_t * g[k]
                gtree_ref[2 * n + 1, k, vs[v]] = jnp.where(flip, g_back, g_front)
                gtree_ref[2 * n + 2, k, vs[v]] = jnp.where(flip, g_front, g_back)
        return carry

    lax.fori_loop(0, inner, split, 0)

    def backward(r, carry):
        gs = [[gtree_ref[inner + r, k, vs[v]] for v in range(nv)] for k in range(3)]
        behind = [gtree_ref[inner + r, 3, vs[v]] for v in range(nv)]
        for s in reversed(range(splats)):
            u = (xpos - row(r, 0, s)) * row(r, 2, s)
            m_y, inv_y = row(r, 1, s), row(r, 3, s)
            ks = [row(r, 7 + k, s) for k in range(3)]
            acc = None
            for v in range(nv):
                alpha = a_ref[r * splats + s, vs[v]]
                trans = t_ref[r * splats + s, vs[v]]
                shade = ks[0] * gs[0][v] + ks[1] * gs[1][v] + ks[2] * gs[2][v]
                diff = shade - behind[v]
                behind[v] = behind[v] + alpha * diff
                weight = trans * alpha
                h = weight * diff
                w = (ypos[v] - m_y) * inv_y
                hw = h * w
                parts = [h, hw, hw * w] + [weight * gs[k][v] for k in range(3)]
                acc = parts if acc is None else [x + y for x, y in zip(acc, parts)]
            hu = acc[0] * u
            sums = [acc[0], hu, acc[1], hu * u, acc[1] * u, acc[2], acc[3], acc[4], acc[5]]
            for p in range(9):
                mbuf[pl.ds((p * splats + s) * 8, 8), :] = sums[p]
        blocks = []
        for p in range(9):
            total = mbuf[pl.ds(p * 64, 8, stride=8), :]
            for j in range(1, 8):
                total = total + mbuf[pl.ds(p * 64 + j, 8, stride=8), :]
            blocks.append(total)
        summed = jnp.dot(
            jnp.concatenate(blocks, 0), gather_out, precision=HI, preferred_element_type=jnp.float32
        )
        mask = x_ref[9, pl.ds(r, 1), :] == rank_row
        for p in range(9):
            red_ref[p, pl.ds(r, 1), :] = jnp.sum(
                jnp.where(mask, summed[p * splats:(p + 1) * splats], 0.0), 0, keepdims=True
            )
        return carry

    lax.fori_loop(0, regions, backward, 0)

    h0, hu, hv, huu, huv, hvv = [red_ref[p] for p in range(6)]
    squash = jnp.tanh(x_ref[4])
    rho = 0.9 * squash
    inv = 1.0 / (1.0 - rho * rho)
    grad_ref[0] = d_ref[2] * inv * (hu - rho * hv)
    grad_ref[1] = d_ref[3] * inv * (hv - rho * hu)
    grad_ref[2] = inv * (huu - rho * huv)
    grad_ref[3] = inv * (hvv - rho * huv)
    hq = inv * (huu - 2.0 * rho * huv + hvv)
    grad_ref[4] = inv * (huv - rho * hq) * (0.9 * (1.0 - squash * squash))
    grad_ref[5] = h0 * jax.nn.sigmoid(-x_ref[5])
    for k in range(3):
        tone = d_ref[7 + k]
        grad_ref[6 + k] = red_ref[6 + k] * tone * (1.0 - tone)


def render(received, flip_rows, wanted, spread):
    regions, group = received.shape[1:]
    rows = wanted.shape[1]
    nodes = 2 * regions - 1
    f32 = jnp.float32
    return pl.pallas_call(
        render_kernel,
        out_shape=(
            jax.ShapeDtypeStruct((rows, LANES), f32),
            jax.ShapeDtypeStruct((9, regions, group), f32),
        ),
        in_specs=[pl.BlockSpec(memory_space=pltpu.VMEM)] * 4,
        out_specs=(pl.BlockSpec(memory_space=pltpu.VMEM),) * 2,
        scratch_shapes=[
            pltpu.VMEM((NPAR, regions, group), f32),
            pltpu.VMEM((regions, NPAR * 8, LANES), f32),
            pltpu.VMEM((regions * 8, rows, LANES), f32),
            pltpu.VMEM((regions * 8, rows, LANES), f32),
            pltpu.VMEM((nodes, 4, rows, LANES), f32),
            pltpu.VMEM((nodes, 4, rows, LANES), f32),
            pltpu.VMEM((9 * 64, LANES), f32),
            pltpu.VMEM((9, regions, group), f32),
        ],
        compiler_params=pltpu.CompilerParams(vmem_limit_bytes=48 * 1024 * 1024),
    )(received, flip_rows, wanted, spread)


def uncertainty(stripe_feats, w_first, b_first, w_second):
    hidden = jax.nn.gelu(
        jnp.dot(stripe_feats, w_first, preferred_element_type=jnp.float32) + b_first
    ).astype(jnp.bfloat16)
    return 0.5 + jax.nn.softplus(jnp.dot(hidden, w_second, preferred_element_type=jnp.float32))


def shards(gaussians, depth, coverage, flips, features, w_first, b_first, w_second, target):
    regions = lax.axis_size("region")
    my_index = lax.axis_index("region")
    tile_count = depth.shape[1]
    splats = depth.shape[2]
    stripe_tiles = tile_count // regions
    group = stripe_tiles * splats
    span = LANES // stripe_tiles
    rows = TSIDE * TSIDE // span

    payload = jnp.concatenate(
        [
            gaussians[0],
            depth.reshape(1, tile_count * splats).astype(jnp.float32),
            jnp.repeat(coverage, splats, axis=1).astype(jnp.float32),
        ],
        0,
    ).reshape(11, regions, group)
    received = lax.all_to_all(payload, "region", 1, 1)
    spread = uncertainty(features, w_first, b_first, w_second)

    def to_rows(x):
        lead = x.shape[:-1]
        x = x.reshape(lead + (stripe_tiles, rows, span))
        return jnp.swapaxes(x, -3, -2).reshape(lead + (rows, LANES))

    my_flips = lax.dynamic_slice_in_dim(flips, my_index * stripe_tiles, stripe_tiles, 0)
    flip_rows = jnp.repeat(my_flips.T.astype(jnp.float32), span, axis=1)[:, None, :]
    loss, grads = render(received, flip_rows, to_rows(target), to_rows(spread))
    pixel_loss = jnp.swapaxes(loss.reshape(rows, stripe_tiles, span), 0, 1).reshape(-1)
    returned = lax.all_to_all(grads, "region", 1, 1)
    return (pixel_loss, returned.reshape(1, 9, tile_count * splats))


def solution(mesh):
    placed = (
        P("region", None, None),
        P("region", None, None),
        P("region", None),
        P(),
        P("region", None),
        P(),
        P(),
        P(),
        P(None, "region"),
    )
    return jax.shard_map(
        shards,
        mesh=mesh,
        in_specs=placed,
        out_specs=(P("region"), P("region", None, None)),
        check_vma=False,
    )
```

profile of v0, /device:TPU:0, one launch (start us, length us, event | category | flops | bytes accessed | tf_op | source)
XLA Modules:
  0.0 65.7 jit_solution(5316300877853353807)
XLA Ops:
  0.6 0.0 copy-start
  0.6 0.9 %convert_element_type.43 = f32[1,512,8]{1,2,0:T(8,128)S(1)} convert(s32[1,512,8]{1,2,0:T(8,128)} %param.10) | non-fusion elementwise | flops 4096 | bytes 32768 | tf_op jit(solution)/shard_map/convert_element_type | solution.py:250
  1.5 0.1 copy.42
  1.6 0.2 convert_element_type.44
  1.8 0.7 %convert_reduce_fusion = f32[512]{0:T(512)S(1)} fusion(s32[1,512]{1,0:T(1,128)} %param.11), kind=kLoop, calls=%fused_computation.16 | loop fusion | flops 512 | bytes 4096 | tf_op jit(solution)/shard_map/convert_element_type | solution.py:251
  2.5 0.1 convert_element_type.46
  2.6 0.1 copy.43
  2.7 0.1 copy.44
  2.7 0.9 %pad_maximum_fusion = f32[11,32,128]{2,1,0:T(8,128)S(1)} fusion(f32[1,32,128]{2,1,0:T(8,128)S(1)} %copy.44, f32[1,32,128]{2,1,0:T(8,128)S(1)} %convert_element_type.44, f32[9,32,128]{2,1,0:T(8,128)} %bitcast.25), kind=kLoop, calls=%fused_computation.10 | loop fusion | flops 90112 | bytes 360448 | tf_op jit(solution)/shard_map/concatenate | solution.py:247
  3.7 0.8 %copy.45 = f32[11,32,128]{2,0,1:T(8,128)} copy(f32[11,32,128]{2,1,0:T(8,128)S(1)} %pad_maximum_fusion) | data formatting | bytes 360448 | tf_op jit(solution)/shard_map/concatenate | solution.py:247
  4.5 7.3 %all-to-all-start = ((f32[11,32,128]{2,0,1:T(8,128)}), f32[11,32,128]{2,0,1:T(8,128)S(1)}, u32[]{:S(2)}, u32[]{:S(2)}) async-start(f32[11,32,128]{2,0,1:T(8,128)} %copy.45), calls=%async_computation | async-start | bytes 524288 | tf_op jit(solution)/shard_map/all_to_all | solution.py:255
  11.8 0.8 %convert_bitcast_fusion = f32[31,16]{1,0:T(8,128)S(1)} fusion(s32[512,31]{0,1:T(8,128)} %param.12, s32[]{:T(128)S(6)} %select_n.7), kind=kLoop, calls=%fused_computation.15 | loop fusion | flops 496 | bytes 3972 | tf_op jit(solution)/shard_map/convert_element_type | solution.py:264
  12.6 0.7 %copy.46 = f32[31,16]{0,1:T(8,128)} copy(f32[31,16]{1,0:T(8,128)S(1)} %convert_bitcast_fusion) | data formatting | bytes 3968 | tf_op jit(solution)/shard_map/convert_element_type | solution.py:264
  13.3 0.7 %reshape.81 = bf16[384,1]{0,1:T(2,128)(2,1)S(1)} reshape(bf16[384]{0:T(512)(128)(2,1)} %param.16) | data formatting | bytes 1536 | tf_op args[7]
  14.0 0.0 copy-done
  14.0 0.0 copy-start.2
  14.0 0.0 copy-start.1
  14.0 5.4 %fusion.8 = f32[1,4096]{1,0:T(1,128)} fusion(bf16[384,1]{0,1:T(2,128)(2,1)S(1)} %reshape.81, bf16[4096,384]{1,0:T(8,128)(2,1)S(1)} %copy-done, bf16[384,384]{1,0:T(8,128)(2,1)} %param.14, f32[384]{0:T(512)} %param.15), kind=kOutput, calls=%fused_computation.9 | convolution fusion | flops 1226833920 | bytes 3459328 | tf_op jit(solution)/shard_map/dot_general | solution.py:234
  19.4 0.0 copy-done.2
  19.4 0.1 copy.50.flip_ref
  19.5 0.0 copy-done.1
  19.5 1.4 %reshape.74 = f32[3,16,32,8]{3,2,1,0:T(8,128)} reshape(f32[3,4096]{1,0:T(4,128)S(1)} %copy-done.1) | data formatting | bytes 98304 | tf_op jit(solution)/shard_map/reshape | solution.py:260
  20.9 2.1 %copy.47 = f32[3,32,16,8]{1,3,2,0:T(8,128)} copy(f32[3,32,16,8]{3,1,2,0:T(8,128)} %bitcast.19) | data formatting | bytes 98304 | tf_op jit(solution)/shard_map/transpose | solution.py:261
  23.0 1.0 %copy.51.wanted_ref = f32[3,32,128]{2,1,0:T(8,128)S(1)} copy(f32[3,32,128]{1,2,0:T(8,128)} %bitcast.21) | data formatting | bytes 98304 | tf_op jit(solution)/shard_map/reshape | solution.py:261
  24.0 0.8 %fusion.9 = f32[4096]{0:T(1024)S(1)} fusion(f32[4096]{0:T(1024)} %bitcast.26), kind=kLoop, calls=%fused_computation.14 | loop fusion | flops 28672 | bytes 32768 | tf_op jit(solution)/shard_map/add | solution.py:234
  24.7 0.9 %reshape.76 = f32[16,32,8]{2,1,0:T(8,128)} reshape(f32[4096]{0:T(1024)S(1)} %fusion.9) | data formatting | bytes 32768 | tf_op jit(solution)/shard_map/reshape | solution.py:260
  25.6 1.1 %copy.48 = f32[32,16,8]{0,2,1:T(8,128)S(1)} copy(f32[32,16,8]{2,0,1:T(8,128)} %bitcast.20) | data formatting | bytes 32768 | tf_op jit(solution)/shard_map/transpose | solution.py:261
  26.7 0.1 copy.52.spread_ref
  26.7 0.0 all-to-all-done
  26.7 0.1 copy.49.x_ref
  26.8 19.9 %shard_map.104 = (f32[32,128]{1,0:T(8,128)S(1)}, f32[9,32,128]{2,1,0:T(8,128)S(1)}) custom-call(f32[11,32,128]{2,1,0:T(8,128)S(1)} %copy.49.x_ref, f32[31,1,128]{2,1,0:T(1,128)S(1)} %copy.50.flip_ref, f32[3,32,128]{2,1,0:T(8,128)S(1)} %copy.51.wanted_ref, f32[32,128]{1,0:T(8,128)S(1)} %copy.52.spread_ref), custom_call_target="tpu_custom_call" | custom-call | tf_op jit(solution)/shard_map/pallas_call | solution.py:208
  46.7 0.8 %copy.55 = f32[9,32,128]{2,0,1:T(8,128)} copy(f32[9,32,128]{2,1,0:T(8,128)S(1)} %get-tuple-element.5) | data formatting | bytes 294912 | tf_op jit(solution)/shard_map/pallas_call | solution.py:208
  47.5 6.0 %all-to-all-start.1 = ((f32[9,32,128]{2,0,1:T(8,128)}), f32[9,32,128]{2,0,1:T(8,128)}, u32[]{:S(2)}, u32[]{:S(2)}) async-start(f32[9,32,128]{2,0,1:T(8,128)} %copy.55), calls=%async_computation.1 | async-start | bytes 524288 | tf_op jit(solution)/shard_map/all_to_all | solution.py:267
  53.5 0.1 copy.53
  53.6 0.1 copy.54
  53.7 0.8 %reshape.79 = f32[4096]{0:T(1024)} reshape(f32[16,32,8]{2,1,0:T(8,128)S(1)} %copy.54) | data formatting | bytes 32768 | tf_op jit(solution)/shard_map/reshape | solution.py:266
  54.5 9.6 %all-to-all-done.1 = f32[9,32,128]{2,0,1:T(8,128)} async-done(((f32[9,32,128]{2,0,1:T(8,128)}), f32[9,32,128]{2,0,1:T(8,128)}, u32[]{:S(2)}, u32[]{:S(2)}) %all-to-all-start.1) | async-done | bytes 147488 | tf_op jit(solution)/shard_map/all_to_all | solution.py:267
  64.0 1.7 %copy.56 = f32[9,32,128]{2,1,0:T(8,128)} copy(f32[9,32,128]{2,0,1:T(8,128)} %all-to-all-done.1) | data formatting | bytes 294912 | tf_op jit(solution)/shard_map/all_to_all | solution.py:267
  (2 shorter events, 0.0 us)
Async XLA Ops:
  0.6 13.4 %copy-start = (bf16[4096,384]{1,0:T(8,128)(2,1)S(1)}, bf16[4096,384]{1,0:T(8,128)(2,1)}, u32[]{:S(2)}) copy-start(bf16[4096,384]{1,0:T(8,128)(2,1)} %param.13) | copy-start | bytes 9437188
  4.5 22.2 %all-to-all-start = ((f32[11,32,128]{2,0,1:T(8,128)}), f32[11,32,128]{2,0,1:T(8,128)S(1)}, u32[]{:S(2)}, u32[]{:S(2)}) async-start(f32[11,32,128]{2,0,1:T(8,128)} %copy.45), calls=%async_computation | async-start | bytes 524288 | tf_op jit(solution)/shard_map/all_to_all | solution.py:255
  14.0 5.5 %copy-start.2 = (f32[31,16]{0,1:T(8,128)S(1)}, f32[31,16]{0,1:T(8,128)}, u32[]{:S(2)}) copy-start(f32[31,16]{0,1:T(8,128)} %copy.46) | copy-start | bytes 5956
  14.0 5.5 %copy-start.1 = (f32[3,4096]{1,0:T(4,128)S(1)}, f32[3,4096]{1,0:T(4,128)}, u32[]{:S(2)}) copy-start(f32[3,4096]{1,0:T(4,128)} %param.17) | copy-start | bytes 147460
  47.5 16.5 %all-to-all-start.1 = ((f32[9,32,128]{2,0,1:T(8,128)}), f32[9,32,128]{2,0,1:T(8,128)}, u32[]{:S(2)}, u32[]{:S(2)}) async-start(f32[9,32,128]{2,0,1:T(8,128)} %copy.55), calls=%async_computation.1 | async-start | bytes 524288 | tf_op jit(solution)/shard_map/all_to_all | solution.py:267
where the time goes:
time: 66.2 us; the launch traced here: 65.7 us
  Pallas kernels  19.9 us (30%)
  starting transfers between devices  13.3 us (20%)
  local copies, waits for them, and re-layouts  12.7 us (19%)
  waiting for transfers between devices  9.56 us (14%)
  matrix products  5.44 us (8%)
  other arithmetic  4.07 us (6%)
  between operations  0.73 us (1%)
    pallas_call x1, Pallas kernels, render(): pl.pallas_call(render_kernel, out_shape=(jax.ShapeDtypeStruct((rows, LANE...  19.9 us
    all_to_all x1, waiting for transfers between devices, shards(): returned = lax.all_to_all(grads, 'region', 1, 1)  9.56 us
    all_to_all x1, starting transfers between devices, shards(): received = lax.all_to_all(payload, 'region', 1, 1)  7.33 us
    all_to_all x1, starting transfers between devices, shards(): returned = lax.all_to_all(grads, 'region', 1, 1)  5.96 us
    dot_general x1, matrix products, uncertainty(): jnp.dot(hidden, w_second, preferred_element_type=jnp.float32)  5.44 us
    transpose x2, local copies, waits for them, and re-layouts, to_rows(): return jnp.swapaxes(x, -3, -2).reshape(lead + (rows, LANES))  3.14 us
    reshape x2, local copies, waits for them, and re-layouts, to_rows(): x = x.reshape(lead + (stripe_tiles, rows, span))  2.24 us
    all_to_all x1, local copies, waits for them, and re-layouts, shards(): returned = lax.all_to_all(grads, 'region', 1, 1)  1.66 us
  transfers between devices with their start and end apart: 2, of which 1 were waited for; matrix products, arithmetic and copies ran while one was open for 24% of the time, Pallas kernels for 0%

commit v1 on v0

--- a/solution.py
+++ b/solution.py
@@ -1,5 +1,3 @@
-import functools
-
 import jax
 import jax.numpy as jnp
 from jax import lax
@@ -14,8 +12,22 @@
 HI = lax.Precision.HIGHEST
 
 
-def render_kernel(
-    x_ref, flip_ref, wanted_ref, spread_ref, loss_ref, grad_ref,
+def dot(x, y, transposed=False):
+    dims = (((1,), (1 if transposed else 0,)), ((), ()))
+    return lax.dot_general(x, y, dims, precision=HI, preferred_element_type=jnp.float32)
+
+
+def same(shape, first, second):
+    left = first(lax.broadcasted_iota(jnp.int32, shape, 0))
+    right = second(lax.broadcasted_iota(jnp.int32, shape, 1))
+    return (left == right).astype(jnp.float32)
+
+
+def splat_kernel(
+    gauss_ref, depth_ref, cover_ref, flips_ref, feat_hbm, first_ref, bias_ref, second_ref,
+    target_ref, loss_ref, out_ref,
+    feat_ref, feat_sem, send_ref, recv_ref, send_sem, recv_sem, gsend_ref, grecv_ref, gsend_sem,
+    grecv_sem, x_ref, flip_ref, spread_ref, wanted_ref,
     d_ref, ex_ref, a_ref, t_ref, tree_ref, gtree_ref, mbuf, red_ref,
 ):
     regions, group = x_ref.shape[1:]
@@ -25,6 +37,102 @@
     stripe_tiles = group // splats
     span = LANES // stripe_tiles
     inner = regions - 1
+    tile_count = depth_ref.shape[0]
+    pixels = TSIDE * TSIDE
+    me = lax.axis_index("region")
+
+    load = pltpu.make_async_copy(feat_hbm, feat_ref, feat_sem)
+    load.start()
+    barrier = pltpu.get_barrier_semaphore()
+
+    def greet(i, carry):
+        pl.semaphore_signal(
+            barrier, inc=1, device_id=(lax.rem(me + i, regions),),
+            device_id_type=pl.DeviceIdType.MESH,
+        )
+        return carry
+
+    lax.fori_loop(1, regions, greet, 0)
+
+    owner = same((regions, tile_count), lambda i: i, lambda j: j // stripe_tiles)
+    pick = same((splats, group), lambda i: i, lambda j: j & (splats - 1))
+    place = same(
+        (tile_count, group), lambda i: i & (stripe_tiles - 1), lambda j: j // splats
+    )
+    rank_rows = dot(owner, dot(depth_ref[...].astype(jnp.float32), pick) * place)
+    cover_rows = dot(owner * cover_ref[...].astype(jnp.float32), place)
+    for d in range(regions):
+        send_ref[d, 0:9, :] = gauss_ref[:, d * group:(d + 1) * group]
+        send_ref[d, 9:10, :] = rank_rows[d:d + 1]
+        send_ref[d, 10:11, :] = cover_rows[d:d + 1]
+    load.wait()
+
+    block = max(16, span)
+    per_block = block // span
+
+    def network(j, carry):
+        feats = feat_ref[:, pl.ds(pl.multiple_of(j * block, block), block), :]
+        feats = feats.reshape(stripe_tiles * block, feat_ref.shape[2])
+        hidden = jax.nn.gelu(
+            jnp.dot(feats, first_ref[...], preferred_element_type=jnp.float32) + bias_ref[...]
+        )
+        hidden = hidden.reshape(stripe_tiles, per_block, span, hidden.shape[-1])
+        for i in range(per_block):
+            part = hidden[:, i].reshape(LANES, hidden.shape[-1]).astype(jnp.bfloat16)
+            logits = lax.dot_general(
+                second_ref[...], part, (((1,), (1,)), ((), ())),
+                preferred_element_type=jnp.float32,
+            )
+            spread_ref[pl.ds(j * per_block + i, 1), :] = logits[0:1]
+        return carry
+
+    steps = pixels // block
+    lax.fori_loop(0, steps // 2, network, 0)
+    pl.semaphore_wait(barrier, regions - 1)
+
+    def exchange(i, src, dst, ssem, rsem):
+        peer = lax.rem(me + i, regions)
+        return pltpu.make_async_remote_copy(
+            src_ref=src.at[peer], dst_ref=dst.at[me], send_sem=ssem.at[peer],
+            recv_sem=rsem.at[me], device_id=(peer,), device_id_type=pl.DeviceIdType.MESH,
+        )
+
+    def arrival(i, src, dst, ssem, rsem):
+        peer = lax.rem(me + i, regions)
+        return pltpu.make_async_remote_copy(
+            src_ref=src.at[peer], dst_ref=dst.at[peer], send_sem=ssem.at[peer],
+            recv_sem=rsem.at[peer], device_id=(peer,), device_id_type=pl.DeviceIdType.MESH,
+        )
+
+    there = (send_ref, recv_ref, send_sem, recv_sem)
+    back_way = (gsend_ref, grecv_ref, gsend_sem, grecv_sem)
+
+    def send(i, carry):
+        exchange(i, *there).start()
+        return carry
+
+    lax.fori_loop(1, regions, send, 0)
+    recv_ref[me] = send_ref[me]
+    lax.fori_loop(steps // 2, steps, network, 0)
+
+    tile_lane = same((LANES, stripe_tiles), lambda i: i // span, lambda j: j)
+    lane_pixel = same((LANES, pixels), lambda i: i & (span - 1), lambda j: j & (span - 1))
+    row_pixel = same((rows, pixels), lambda i: i, lambda j: j // span)
+    for k in range(3):
+        flat = jnp.concatenate(
+            [target_ref[k:k + 1, t * pixels:(t + 1) * pixels] for t in range(stripe_tiles)], 0
+        )
+        wanted_ref[k] = dot(row_pixel, dot(tile_lane, flat) * lane_pixel, True)
+    lane_tile = same((stripe_tiles, LANES), lambda i: i, lambda j: j // span)
+    flip_ref[...] = dot(flips_ref[...], lane_tile)
+
+    def arrive(i, carry):
+        arrival(i, *there).wait()
+        return carry
+
+    lax.fori_loop(1, regions, arrive, 0)
+    for p in range(11):
+        x_ref[p] = recv_ref[:, p, :]
 
     sub = lax.broadcasted_iota(jnp.int32, (8, LANES), 0)
     lane = lax.broadcasted_iota(jnp.int32, (8, LANES), 1)
@@ -99,7 +207,7 @@
 
     def merge(i, carry):
         n = inner - 1 - i
-        flip = jnp.broadcast_to(flip_ref[n], (8, LANES)) > 0.0
+        flip = jnp.broadcast_to(flip_ref[pl.ds(n, 1), :], (8, LANES)) > 0.0
         for v in range(nv):
             low = [tree_ref[2 * n + 1, k, vs[v]] for k in range(4)]
             high = [tree_ref[2 * n + 2, k, vs[v]] for k in range(4)]
@@ -112,20 +220,28 @@
 
     lax.fori_loop(0, inner, merge, 0)
 
+    losses = []
     for v in range(nv):
-        spread = spread_ref[vs[v]]
+        logit = spread_ref[vs[v]]
+        spread = 0.5 + jnp.maximum(logit, 0.0) + jnp.log1p(jnp.exp(-jnp.abs(logit)))
         inv_square = 1.0 / (spread * spread)
         clear = tree_ref[0, 3, vs[v]]
         residual = [tree_ref[0, k, vs[v]] + clear - wanted_ref[k, vs[v]] for k in range(3)]
         total = residual[0] * residual[0] + residual[1] * residual[1] + residual[2] * residual[2]
-        loss_ref[vs[v]] = 0.5 * total * inv_square + jnp.log(spread)
+        losses.append(0.5 * total * inv_square + jnp.log(spread))
         gs = [res * inv_square for res in residual]
         for k in range(3):
             gtree_ref[0, k, vs[v]] = gs[k]
         gtree_ref[0, 3, vs[v]] = gs[0] + gs[1] + gs[2]
 
+    pixel_row = same((pixels, rows), lambda i: i // span, lambda j: j)
+    pixel_lane = same((pixels, LANES), lambda i: i & (span - 1), lambda j: j & (span - 1))
+    flat = dot(lane_tile, dot(pixel_row, jnp.concatenate(losses, 0)) * pixel_lane, True)
+    for t in range(stripe_tiles):
+        loss_ref[0:1, t * pixels:(t + 1) * pixels] = flat[t:t + 1]
+
     def split(n, carry):
-        flip = jnp.broadcast_to(flip_ref[n], (8, LANES)) > 0.0
+        flip = jnp.broadcast_to(flip_ref[pl.ds(n, 1), :], (8, LANES)) > 0.0
         for v in range(nv):
             low = [tree_ref[2 * n + 1, k, vs[v]] for k in range(4)]
             high = [tree_ref[2 * n + 2, k, vs[v]] for k in range(4)]
@@ -182,38 +298,95 @@
             )
         return carry
 
-    lax.fori_loop(0, regions, backward, 0)
-
-    h0, hu, hv, huu, huv, hvv = [red_ref[p] for p in range(6)]
-    squash = jnp.tanh(x_ref[4])
-    rho = 0.9 * squash
-    inv = 1.0 / (1.0 - rho * rho)
-    grad_ref[0] = d_ref[2] * inv * (hu - rho * hv)
-    grad_ref[1] = d_ref[3] * inv * (hv - rho * hu)
-    grad_ref[2] = inv * (huu - rho * huv)
-    grad_ref[3] = inv * (hvv - rho * huv)
-    hq = inv * (huu - 2.0 * rho * huv + hvv)
-    grad_ref[4] = inv * (huv - rho * hq) * (0.9 * (1.0 - squash * squash))
-    grad_ref[5] = h0 * jax.nn.sigmoid(-x_ref[5])
-    for k in range(3):
-        tone = d_ref[7 + k]
-        grad_ref[6 + k] = red_ref[6 + k] * tone * (1.0 - tone)
-
-
-def render(received, flip_rows, wanted, spread):
-    regions, group = received.shape[1:]
-    rows = wanted.shape[1]
+    batch = 8
+    batches = regions // batch
+
+    def finish(i, carry):
+        which = lax.rem(i + 1 + me // batch, batches)
+        base = pl.multiple_of(which * batch, batch)
+        lax.fori_loop(base, base + batch, backward, 0)
+        some = pl.ds(base, batch)
+        h0, hu, hv, huu, huv, hvv = [red_ref[p, some, :] for p in range(6)]
+        squash = jnp.tanh(x_ref[4, some, :])
+        rho = 0.9 * squash
+        inv = 1.0 / (1.0 - rho * rho)
+        hq = inv * (huu - 2.0 * rho * huv + hvv)
+        results = [
+            d_ref[2, some, :] * inv * (hu - rho * hv),
+            d_ref[3, some, :] * inv * (hv - rho * hu),
+            inv * (huu - rho * huv),
+            inv * (hvv - rho * huv),
+            inv * (huv - rho * hq) * (0.9 * (1.0 - squash * squash)),
+            h0 * jax.nn.sigmoid(-x_ref[5, some, :]),
+        ]
+        for k in range(3):
+            tone = d_ref[7 + k, some, :]
+            results.append(red_ref[6 + k, some, :] * tone * (1.0 - tone))
+        for j in range(batch):
+            gsend_ref[base + j, 0:9, :] = jnp.concatenate([x[j:j + 1] for x in results], 0)
+        for j in range(batch):
+            peer = base + j
+
+            @pl.when(peer != me)
+            def _():
+                pltpu.make_async_remote_copy(
+                    src_ref=gsend_ref.at[peer], dst_ref=grecv_ref.at[me],
+                    send_sem=gsend_sem.at[peer], recv_sem=grecv_sem.at[me],
+                    device_id=(peer,), device_id_type=pl.DeviceIdType.MESH,
+                ).start()
+
+        return carry
+
+    lax.fori_loop(0, batches, finish, 0)
+    grecv_ref[me] = gsend_ref[me]
+
+    def collect(i, carry):
+        arrival(i, *back_way).wait()
+        return carry
+
+    lax.fori_loop(1, regions, collect, 0)
+    for d in range(regions):
+        out_ref[:, d * group:(d + 1) * group] = grecv_ref[d, 0:9, :]
+
+
+def shards(gaussians, depth, coverage, flips, features, w_first, b_first, w_second, target):
+    regions = lax.axis_size("region")
+    my_index = lax.axis_index("region")
+    tile_count = depth.shape[1]
+    splats = depth.shape[2]
+    stripe_tiles = tile_count // regions
+    group = stripe_tiles * splats
+    pixels = TSIDE * TSIDE
+    rows = pixels * stripe_tiles // LANES
     nodes = 2 * regions - 1
+    width = features.shape[1]
     f32 = jnp.float32
-    return pl.pallas_call(
-        render_kernel,
+    my_flips = lax.dynamic_slice_in_dim(flips, my_index * stripe_tiles, stripe_tiles, 0)
+    vmem = pl.BlockSpec(memory_space=pltpu.VMEM)
+    dma = pltpu.SemaphoreType.DMA
+    loss, grads = pl.pallas_call(
+        splat_kernel,
         out_shape=(
-            jax.ShapeDtypeStruct((rows, LANES), f32),
-            jax.ShapeDtypeStruct((9, regions, group), f32),
+            jax.ShapeDtypeStruct((1, stripe_tiles * pixels), f32),
+            jax.ShapeDtypeStruct((9, tile_count * splats), f32),
         ),
-        in_specs=[pl.BlockSpec(memory_space=pltpu.VMEM)] * 4,
-        out_specs=(pl.BlockSpec(memory_space=pltpu.VMEM),) * 2,
+        in_specs=[vmem] * 4 + [pl.BlockSpec(memory_space=pl.ANY)] + [vmem] * 4,
+        out_specs=(vmem, vmem),
         scratch_shapes=[
+            pltpu.VMEM((stripe_tiles, pixels, width), features.dtype),
+            dma(()),
+            pltpu.VMEM((regions, 16, group), f32),
+            pltpu.VMEM((regions, 16, group), f32),
+            dma((regions,)),
+            dma((regions,)),
+            pltpu.VMEM((regions, 16, group), f32),
+            pltpu.VMEM((regions, 16, group), f32),
+            dma((regions,)),
+            dma((regions,)),
+            pltpu.VMEM((11, regions, group), f32),
+            pltpu.VMEM((regions - 1, LANES), f32),
+            pltpu.VMEM((rows, LANES), f32),
+            pltpu.VMEM((3, rows, LANES), f32),
             pltpu.VMEM((NPAR, regions, group), f32),
             pltpu.VMEM((regions, NPAR * 8, LANES), f32),
             pltpu.VMEM((regions * 8, rows, LANES), f32),
@@ -223,49 +396,21 @@
             pltpu.VMEM((9 * 64, LANES), f32),
             pltpu.VMEM((9, regions, group), f32),
         ],
-        compiler_params=pltpu.CompilerParams(vmem_limit_bytes=48 * 1024 * 1024),
-    )(received, flip_rows, wanted, spread)
-
-
-def uncertainty(stripe_feats, w_first, b_first, w_second):
-    hidden = jax.nn.gelu(
-        jnp.dot(stripe_feats, w_first, preferred_element_type=jnp.float32) + b_first
-    ).astype(jnp.bfloat16)
-    return 0.5 + jax.nn.softplus(jnp.dot(hidden, w_second, preferred_element_type=jnp.float32))
-
-
-def shards(gaussians, depth, coverage, flips, features, w_first, b_first, w_second, target):
-    regions = lax.axis_size("region")
-    my_index = lax.axis_index("region")
-    tile_count = depth.shape[1]
-    splats = depth.shape[2]
-    stripe_tiles = tile_count // regions
-    group = stripe_tiles * splats
-    span = LANES // stripe_tiles
-    rows = TSIDE * TSIDE // span
-
-    payload = jnp.concatenate(
-        [
-            gaussians[0],
-            depth.reshape(1, tile_count * splats).astype(jnp.float32),
-            jnp.repeat(coverage, splats, axis=1).astype(jnp.float32),
-        ],
-        0,
-    ).reshape(11, regions, group)
-    received = lax.all_to_all(payload, "region", 1, 1)
-    spread = uncertainty(features, w_first, b_first, w_second)
-
-    def to_rows(x):
-        lead = x.shape[:-1]
-        x = x.reshape(lead + (stripe_tiles, rows, span))
-        return jnp.swapaxes(x, -3, -2).reshape(lead + (rows, LANES))
-
-    my_flips = lax.dynamic_slice_in_dim(flips, my_index * stripe_tiles, stripe_tiles, 0)
-    flip_rows = jnp.repeat(my_flips.T.astype(jnp.float32), span, axis=1)[:, None, :]
-    loss, grads = render(received, flip_rows, to_rows(target), to_rows(spread))
-    pixel_loss = jnp.swapaxes(loss.reshape(rows, stripe_tiles, span), 0, 1).reshape(-1)
-    returned = lax.all_to_all(grads, "region", 1, 1)
-    return (pixel_loss, returned.reshape(1, 9, tile_count * splats))
+        compiler_params=pltpu.CompilerParams(
+            vmem_limit_bytes=56 * 1024 * 1024, collective_id=0, has_side_effects=True
+        ),
+    )(
+        gaussians[0],
+        depth[0],
+        coverage,
+        my_flips.T.astype(f32),
+        features.reshape(stripe_tiles, pixels, width),
+        w_first,
+        b_first[None],
+        jnp.broadcast_to(w_second[None], (16, width)),
+        target,
+    )
+    return (loss.reshape(-1), grads[None])
 
 
 def solution(mesh):

time: 66.2 us -> 55.2 us (0.83)
  Pallas kernels: 19.9 us -> 43.9 us
  starting transfers between devices: 13.3 us -> 0 us
  waiting for transfers between devices: 9.56 us -> 0 us
  matrix products: 5.44 us -> 0 us
  local copies, waits for them, and re-layouts: 12.7 us -> 8.85 us
  other arithmetic: 4.07 us -> 1.4 us
    pallas_call x1, Pallas kernels: 19.9 us -> 43.9 us  [shards(): pl.pallas_call(splat_kernel, out_shape=(jax.ShapeDtypeStruct((1, stripe_t...]
    all_to_all x2 -> x0, starting transfers between devices: 13.3 us -> none  [the longest x1 7.33 us: shards(): received = lax.all_to_all(payload, 'region', 1, 1)]
    all_to_all x2 -> x0, waiting for transfers between devices: 9.56 us -> none  [the longest x1 9.56 us: shards(): returned = lax.all_to_all(grads, 'region', 1, 1)]
    unnamed x7 -> x4, local copies, waits for them, and re-layouts: 0.7 us -> 6.32 us
    dot_general x1 -> x0, matrix products: 5.44 us -> none  [uncertainty(): jnp.dot(hidden, w_second, preferred_element_type=jnp.float32)]
    reshape x5 -> x0, local copies, waits for them, and re-layouts: 4.08 us -> none  [the longest x2 2.24 us: to_rows(): x = x.reshape(lead + (stripe_tiles, rows, span))]
    transpose x3 -> x0, local copies, waits for them, and re-layouts: 3.26 us -> none  [the longest x2 3.14 us: to_rows(): return jnp.swapaxes(x, -3, -2).reshape(lead + (rows, LANES))]
    broadcast_in_dim x0 -> x2, local copies, waits for them, and re-layouts: none -> 2.53 us  [the longest x1 1.28 us: shards(): jnp.broadcast_to(w_second[None], (16, width))]
  transfers between devices with their start and end apart: 2 -> 0, of which waited for: 1 -> 0; matrix products, arithmetic and copies ran while one was open for 24% -> 0% of each run, Pallas kernels for 0% -> 0%
where the time goes in v1:
time: 55.2 us; the launch traced here: 54.8 us
  Pallas kernels  43.9 us (80%)
  local copies, waits for them, and re-layouts  8.85 us (16%)
  other arithmetic  1.4 us (3%)
  between operations  0.64 us (1%)
    pallas_call x1, Pallas kernels, shards(): pl.pallas_call(splat_kernel, out_shape=(jax.ShapeDtypeStruct((1, stripe_t...  43.9 us
    unnamed x4, local copies, waits for them, and re-layouts  6.32 us
    convert_element_type x1, other arithmetic, shards(): my_flips.T.astype(f32)  1.4 us
    broadcast_in_dim x1, local copies, waits for them, and re-layouts, shards(): jnp.broadcast_to(w_second[None], (16, width))  1.28 us
    broadcast_in_dim x1, local copies, waits for them, and re-layouts, shards(): b_first[None]  1.25 us

profile of v1, /device:TPU:0, one launch (start us, length us, event | category | flops | bytes accessed | tf_op | source)
XLA Modules:
  0.0 54.8 jit_solution(3440110065636735555)
XLA Ops:
  0.6 1.2 %broadcast_in_dim.12.bias_ref = f32[1,384]{1,0:T(1,128)} reshape(f32[384]{0:T(512)} %param.15) | data formatting | bytes 3072 | tf_op jit(solution)/shard_map/broadcast_in_dim | solution.py:409
  1.9 1.3 %broadcast_in_dim.13.second_ref = bf16[16,384]{1,0:T(8,128)(2,1)} broadcast(bf16[384]{0:T(512)(128)(2,1)} %param.16), dimensions={1} | broadcast | bytes 13056 | tf_op jit(solution)/shard_map/broadcast_in_dim | solution.py:410
  3.2 1.4 %convert_bitcast_fusion.flips_ref = f32[31,16]{1,0:T(8,128)} fusion(s32[512,31]{0,1:T(8,128)} %param.12, s32[]{:T(128)S(6)} %select_n.3), kind=kLoop, calls=%fused_computation.1 | loop fusion | flops 496 | bytes 3972 | tf_op jit(solution)/shard_map/convert_element_type | solution.py:406
  4.6 1.7 %copy.15 = f32[1,9,4096]{2,1,0:T(8,128)} copy(f32[1,9,4096]{2,0,1:T(1,128)} %param.9) | data formatting | bytes 294912
  6.2 1.5 %copy.11 = s32[1,512,8]{2,1,0:T(8,128)} copy(s32[1,512,8]{1,2,0:T(8,128)} %param.10) | data formatting | bytes 32768 | tf_op args[1]
  7.8 43.9 %shard_map.104 = (f32[1,4096]{1,0:T(1,128)}, f32[9,4096]{1,0:T(8,128)}) custom-call(f32[9,4096]{1,0:T(8,128)} %bitcast.10, s32[512,8]{1,0:T(8,128)} %bitcast.11, s32[1,512]{1,0:T(1,128)} %cover_ref.1, f32[31,16]{1,0:T(8,128)} %convert_bitcast_fusion.flips_ref, bf16[16,256,384]{2,1,0:T(8,128)(2,1)} %bitcast.9, bf16[384,384]{1,0:T(8,128)(2,1)} %first_ref.1, ...), custom_call_target="tpu_custom_call" | custom-call | tf_op jit(solution)/shard_map/pallas_call | solution.py:367
  51.7 1.8 %copy.12 = f32[1,9,4096]{2,0,1:T(1,128)} copy(f32[1,9,4096]{2,1,0:T(8,128)} %bitcast.12) | data formatting | bytes 294912
  53.5 1.3 %copy.17 = f32[4096]{0:T(1024)} copy(f32[4096]{0:T(1024)} %bitcast.13) | data formatting | bytes 32768

commit v2 on v1

--- a/solution.py
+++ b/solution.py
@@ -12,9 +12,19 @@
 HI = lax.Precision.HIGHEST
 
 
-def dot(x, y, transposed=False):
+def dot(x, y, transposed=False, selector=1):
     dims = (((1,), (1 if transposed else 0,)), ((), ()))
-    return lax.dot_general(x, y, dims, precision=HI, preferred_element_type=jnp.float32)
+    bf16 = jnp.bfloat16
+    sel, val = (y, x) if selector == 1 else (x, y)
+    sel = sel.astype(bf16)
+    total = None
+    for _ in range(3):
+        piece = val.astype(bf16)
+        val = val - piece.astype(jnp.float32)
+        pair = (piece, sel) if selector == 1 else (sel, piece)
+        part = lax.dot_general(*pair, dims, preferred_element_type=jnp.float32)
+        total = part if total is None else total + part
+    return total
 
 
 def same(shape, first, second):
@@ -28,7 +38,7 @@
     target_ref, loss_ref, out_ref,
     feat_ref, feat_sem, send_ref, recv_ref, send_sem, recv_sem, gsend_ref, grecv_ref, gsend_sem,
     grecv_sem, x_ref, flip_ref, spread_ref, wanted_ref,
-    d_ref, ex_ref, a_ref, t_ref, tree_ref, gtree_ref, mbuf, red_ref,
+    d_ref, ex_ref, a_ref, t_ref, tree_ref, gtree_ref, mbuf, sum_ref, red_ref,
 ):
     regions, group = x_ref.shape[1:]
     splats = 8
@@ -37,7 +47,7 @@
     stripe_tiles = group // splats
     span = LANES // stripe_tiles
     inner = regions - 1
-    tile_count = depth_ref.shape[0]
+    tile_count = depth_ref.shape[1]
     pixels = TSIDE * TSIDE
     me = lax.axis_index("region")
 
@@ -55,16 +65,30 @@
     lax.fori_loop(1, regions, greet, 0)
 
     owner = same((regions, tile_count), lambda i: i, lambda j: j // stripe_tiles)
-    pick = same((splats, group), lambda i: i, lambda j: j & (splats - 1))
     place = same(
         (tile_count, group), lambda i: i & (stripe_tiles - 1), lambda j: j // splats
     )
-    rank_rows = dot(owner, dot(depth_ref[...].astype(jnp.float32), pick) * place)
-    cover_rows = dot(owner * cover_ref[...].astype(jnp.float32), place)
+    marks = [owner * depth_ref[g:g + 1, :].astype(jnp.float32) for g in range(splats)]
+    marks.append(owner * cover_ref[...].astype(jnp.float32))
+    marked = jnp.dot(
+        jnp.concatenate(marks, 0).astype(jnp.bfloat16), place.astype(jnp.bfloat16),
+        preferred_element_type=jnp.float32,
+    )
+    which_splat = lax.broadcasted_iota(jnp.int32, (regions, group), 1) & (splats - 1)
+    rank_rows = jnp.zeros((regions, group), jnp.float32)
+    for g in range(splats):
+        rank_rows = jnp.where(which_splat == g, marked[g * regions:(g + 1) * regions], rank_rows)
+    cover_rows = marked[splats * regions:]
     for d in range(regions):
-        send_ref[d, 0:9, :] = gauss_ref[:, d * group:(d + 1) * group]
+        for p in range(9):
+            send_ref[d, p:p + 1, :] = gauss_ref[p, :, d * group:(d + 1) * group]
         send_ref[d, 9:10, :] = rank_rows[d:d + 1]
         send_ref[d, 10:11, :] = cover_rows[d:d + 1]
+    bias = bias_ref[...].reshape(1, bias_ref.shape[0])
+    second = jnp.broadcast_to(
+        second_ref[...].astype(jnp.float32).reshape(1, second_ref.shape[0]),
+        (16, second_ref.shape[0]),
+    ).astype(jnp.bfloat16)
     load.wait()
 
     block = max(16, span)
@@ -74,20 +98,20 @@
         feats = feat_ref[:, pl.ds(pl.multiple_of(j * block, block), block), :]
         feats = feats.reshape(stripe_tiles * block, feat_ref.shape[2])
         hidden = jax.nn.gelu(
-            jnp.dot(feats, first_ref[...], preferred_element_type=jnp.float32) + bias_ref[...]
+            jnp.dot(feats, first_ref[...], preferred_element_type=jnp.float32) + bias
         )
         hidden = hidden.reshape(stripe_tiles, per_block, span, hidden.shape[-1])
         for i in range(per_block):
             part = hidden[:, i].reshape(LANES, hidden.shape[-1]).astype(jnp.bfloat16)
             logits = lax.dot_general(
-                second_ref[...], part, (((1,), (1,)), ((), ())),
+                second, part, (((1,), (1,)), ((), ())),
                 preferred_element_type=jnp.float32,
             )
             spread_ref[pl.ds(j * per_block + i, 1), :] = logits[0:1]
         return carry
 
     steps = pixels // block
-    lax.fori_loop(0, steps // 2, network, 0)
+    lax.fori_loop(0, steps // 2, network, 0, unroll=2)
     pl.semaphore_wait(barrier, regions - 1)
 
     def exchange(i, src, dst, ssem, rsem):
@@ -113,7 +137,7 @@
 
     lax.fori_loop(1, regions, send, 0)
     recv_ref[me] = send_ref[me]
-    lax.fori_loop(steps // 2, steps, network, 0)
+    lax.fori_loop(steps // 2, steps, network, 0, unroll=2)
 
     tile_lane = same((LANES, stripe_tiles), lambda i: i // span, lambda j: j)
     lane_pixel = same((LANES, pixels), lambda i: i & (span - 1), lambda j: j & (span - 1))
@@ -122,9 +146,15 @@
         flat = jnp.concatenate(
             [target_ref[k:k + 1, t * pixels:(t + 1) * pixels] for t in range(stripe_tiles)], 0
         )
-        wanted_ref[k] = dot(row_pixel, dot(tile_lane, flat) * lane_pixel, True)
+        wanted_ref[k] = dot(row_pixel, dot(tile_lane, flat, selector=0) * lane_pixel, True, selector=0)
     lane_tile = same((stripe_tiles, LANES), lambda i: i, lambda j: j // span)
-    flip_ref[...] = dot(flips_ref[...], lane_tile)
+    my_tiles = same(
+        (tile_count, LANES), lambda i: i - me * stripe_tiles, lambda j: j // span
+    ).astype(jnp.bfloat16)
+    flip_ref[...] = jnp.dot(
+        flips_ref[...].astype(jnp.float32).astype(jnp.bfloat16), my_tiles,
+        preferred_element_type=jnp.float32,
+    )
 
     def arrive(i, carry):
         arrival(i, *there).wait()
@@ -169,12 +199,10 @@
             jnp.where(mask, jnp.broadcast_to(d_ref[p, pl.ds(r, 1), :], (splats, group)), 0.0)
             for p in range(NPAR)
         ]
-        ex_ref[r] = jnp.dot(
-            jnp.concatenate(picked, 0), spread_in, precision=HI, preferred_element_type=jnp.float32
-        )
-        return carry
-
-    lax.fori_loop(0, regions, expand, 0, unroll=2)
+        ex_ref[r] = dot(jnp.concatenate(picked, 0), spread_in)
+        return carry
+
+    lax.fori_loop(0, regions, expand, 0, unroll=4)
 
     def row(r, p, s):
         return ex_ref[r, pl.ds(p * splats + s, 1), :]
@@ -236,7 +264,7 @@
 
     pixel_row = same((pixels, rows), lambda i: i // span, lambda j: j)
     pixel_lane = same((pixels, LANES), lambda i: i & (span - 1), lambda j: j & (span - 1))
-    flat = dot(lane_tile, dot(pixel_row, jnp.concatenate(losses, 0)) * pixel_lane, True)
+    flat = dot(lane_tile, dot(pixel_row, jnp.concatenate(losses, 0), selector=0) * pixel_lane, True, selector=0)
     for t in range(stripe_tiles):
         loss_ref[0:1, t * pixels:(t + 1) * pixels] = flat[t:t + 1]
 
@@ -282,20 +310,11 @@
             sums = [acc[0], hu, acc[1], hu * u, acc[1] * u, acc[2], acc[3], acc[4], acc[5]]
             for p in range(9):
                 mbuf[pl.ds((p * splats + s) * 8, 8), :] = sums[p]
-        blocks = []
         for p in range(9):
             total = mbuf[pl.ds(p * 64, 8, stride=8), :]
             for j in range(1, 8):
                 total = total + mbuf[pl.ds(p * 64 + j, 8, stride=8), :]
-            blocks.append(total)
-        summed = jnp.dot(
-            jnp.concatenate(blocks, 0), gather_out, precision=HI, preferred_element_type=jnp.float32
-        )
-        mask = x_ref[9, pl.ds(r, 1), :] == rank_row
-        for p in range(9):
-            red_ref[p, pl.ds(r, 1), :] = jnp.sum(
-                jnp.where(mask, summed[p * splats:(p + 1) * splats], 0.0), 0, keepdims=True
-            )
+            sum_ref[lax.rem(r, 8), p * splats:(p + 1) * splats, :] = total
         return carry
 
     batch = 8
@@ -305,6 +324,14 @@
         which = lax.rem(i + 1 + me // batch, batches)
         base = pl.multiple_of(which * batch, batch)
         lax.fori_loop(base, base + batch, backward, 0)
+        summed = dot(sum_ref[...].reshape(batch * 9 * splats, LANES), gather_out)
+        for j in range(batch):
+            mask = x_ref[9, pl.ds(base + j, 1), :] == rank_row
+            for p in range(9):
+                first = (j * 9 + p) * splats
+                red_ref[p, pl.ds(base + j, 1), :] = jnp.sum(
+                    jnp.where(mask, summed[first:first + splats], 0.0), 0, keepdims=True
+                )
         some = pl.ds(base, batch)
         h0, hu, hv, huu, huv, hvv = [red_ref[p, some, :] for p in range(6)]
         squash = jnp.tanh(x_ref[4, some, :])
@@ -346,12 +373,17 @@
 
     lax.fori_loop(1, regions, collect, 0)
     for d in range(regions):
-        out_ref[:, d * group:(d + 1) * group] = grecv_ref[d, 0:9, :]
+        for p in range(9):
+            out_ref[p, :, d * group:(d + 1) * group] = grecv_ref[d, p:p + 1, :]
+
+
+def hand_over(loss_in, grads_in, loss_out, grads_out):
+    loss_out[...] = loss_in[...]
+    grads_out[...] = grads_in[...]
 
 
 def shards(gaussians, depth, coverage, flips, features, w_first, b_first, w_second, target):
     regions = lax.axis_size("region")
-    my_index = lax.axis_index("region")
     tile_count = depth.shape[1]
     splats = depth.shape[2]
     stripe_tiles = tile_count // regions
@@ -361,14 +393,13 @@
     nodes = 2 * regions - 1
     width = features.shape[1]
     f32 = jnp.float32
-    my_flips = lax.dynamic_slice_in_dim(flips, my_index * stripe_tiles, stripe_tiles, 0)
     vmem = pl.BlockSpec(memory_space=pltpu.VMEM)
     dma = pltpu.SemaphoreType.DMA
     loss, grads = pl.pallas_call(
         splat_kernel,
         out_shape=(
             jax.ShapeDtypeStruct((1, stripe_tiles * pixels), f32),
-            jax.ShapeDtypeStruct((9, tile_count * splats), f32),
+            jax.ShapeDtypeStruct((9, 1, tile_count * splats), f32),
         ),
         in_specs=[vmem] * 4 + [pl.BlockSpec(memory_space=pl.ANY)] + [vmem] * 4,
         out_specs=(vmem, vmem),
@@ -394,23 +425,32 @@
             pltpu.VMEM((nodes, 4, rows, LANES), f32),
             pltpu.VMEM((nodes, 4, rows, LANES), f32),
             pltpu.VMEM((9 * 64, LANES), f32),
+            pltpu.VMEM((8, 9 * 8, LANES), f32),
             pltpu.VMEM((9, regions, group), f32),
         ],
         compiler_params=pltpu.CompilerParams(
             vmem_limit_bytes=56 * 1024 * 1024, collective_id=0, has_side_effects=True
         ),
     )(
-        gaussians[0],
-        depth[0],
+        jnp.swapaxes(gaussians, 0, 1),
+        depth[0].T,
         coverage,
-        my_flips.T.astype(f32),
+        flips.T,
         features.reshape(stripe_tiles, pixels, width),
         w_first,
-        b_first[None],
-        jnp.broadcast_to(w_second[None], (16, width)),
+        b_first,
+        w_second,
         target,
     )
-    return (loss.reshape(-1), grads[None])
+    loss, grads = pl.pallas_call(
+        hand_over,
+        out_shape=(
+            jax.ShapeDtypeStruct(loss.shape, f32), jax.ShapeDtypeStruct(grads.shape, f32)
+        ),
+        in_specs=[vmem] * 2,
+        out_specs=(vmem, vmem),
+    )(loss, grads)
+    return (loss.reshape(-1), jnp.swapaxes(grads, 0, 1))
 
 
 def solution(mesh):

time: 55.2 us -> 39.7 us (0.72)
  local copies, waits for them, and re-layouts: 8.85 us -> 0 us
  Pallas kernels: 43.9 us -> 38.8 us
  other arithmetic: 1.4 us -> 0 us
    pallas_call x1, Pallas kernels: 43.9 us -> 37.2 us  [shards(): pl.pallas_call(splat_kernel, out_shape=(jax.ShapeDtypeStruct((1, stripe_t...]
    unnamed x4 -> x0, local copies, waits for them, and re-layouts: 6.32 us -> none
    broadcast_in_dim x2 -> x0, local copies, waits for them, and re-layouts: 2.53 us -> none  [the longest x1 1.28 us: shards(): jnp.broadcast_to(w_second[None], (16, width))]
    pallas_call x0 -> x1, Pallas kernels: none -> 1.6 us  [shards(): pl.pallas_call(hand_over, out_shape=(jax.ShapeDtypeStruct(loss.shape, f32...]
    convert_element_type x1 -> x0, other arithmetic: 1.4 us -> none  [shards(): my_flips.T.astype(f32)]
where the time goes in v2:
time: 39.7 us; the launch traced here: 39.5 us
  Pallas kernels  38.8 us (98%)
  between operations  0.64 us (2%)
    pallas_call x1, Pallas kernels, shards(): pl.pallas_call(splat_kernel, out_shape=(jax.ShapeDtypeStruct((1, stripe_t...  37.2 us
    pallas_call x1, Pallas kernels, shards(): pl.pallas_call(hand_over, out_shape=(jax.ShapeDtypeStruct(loss.shape, f32...  1.6 us

profile of v2, /device:TPU:0, one launch (start us, length us, event | category | flops | bytes accessed | tf_op | source)
XLA Modules:
  0.0 39.5 jit_solution(2012781403937567005)
XLA Ops:
  0.6 37.2 %shard_map.104 = (f32[1,4096]{1,0:T(1,128)}, f32[9,1,4096]{2,1,0:T(1,128)}) custom-call(f32[9,1,4096]{2,1,0:T(1,128)} %bitcast.9, s32[8,512]{1,0:T(8,128)} %bitcast.11, s32[1,512]{1,0:T(1,128)} %cover_ref.1, s32[31,512]{1,0:T(8,128)} %bitcast.10, bf16[16,256,384]{2,1,0:T(8,128)(2,1)} %bitcast.8, bf16[384,384]{1,0:T(8,128)(2,1)} %first_ref.1, f32[384]{0:T(512)} %bias_ref.1, ...), custom_call_target="tpu_custom_call" | custom-call | tf_op jit(solution)/shard_map/pallas_call | solution.py:398
  37.9 1.6 %shard_map.105 = (f32[1,4096]{1,0:T(1,128)}, f32[9,1,4096]{2,1,0:T(1,128)}) custom-call(f32[1,4096]{1,0:T(1,128)} %get-tuple-element.6.loss_in, f32[9,1,4096]{2,1,0:T(1,128)} %get-tuple-element.7.grads_in), custom_call_target="tpu_custom_call" | custom-call | tf_op jit(solution)/shard_map/pallas_call | solution.py:445
